TPU v7x, 512 devices: a whole 4x4x16 slice. The times are simulated.
512 devices in a mesh: uv: 64 (over z, y), freq: 8 (over x, core).
Axes of the slice: x: 4, y: 4, z: 16, core: 2. Of those that a mesh axis runs over, the one named last changes fastest.
Arguments:
- model_image: bfloat16 [2048, 2048], P('uv'), may hold values from -6 to 6
- visibilities: float32 [2, 64, 8, 64, 32], P(None, 'uv', 'freq'), may hold values from -6 to 6
- cell_rows: int32 [64, 8, 64, 32], P('uv', 'freq'), may hold values from 0 to 31
- cell_cols: int32 [64, 8, 64, 32], P('uv', 'freq'), may hold values from 0 to 2047
- kernel_offsets: int32 [2, 64, 8, 64, 32], P(None, 'uv', 'freq'), may hold values from 0 to 127
- slot_counts: int32 [64, 8, 64], P('uv', 'freq'), may hold values from 1 to 32, as said below
- kernel_table: float32 [128, 8], replicated, may hold values from 0.05 to 1
Outputs:
- residual_vis: float32 [2, 64, 8, 64, 32], P(None, 'uv', 'freq')
- gradient: float32 [2048, 2048], P('uv', 'freq')
Inputs may be any that keep to these rules, and one draw needn't show every extreme that they name: Slots 0 .. slot_counts - 1 of a sender tile, group and destination tile are live; in every draw some destination tile receives 32 live slots from every sender tile of every group.
All inputs are finite; a program needn't handle non-finite values.
Results may differ from a plain program's by a relative error of at most 0.013.
Values may be sent and summed in bfloat16 or wider, within the bound.
A program may use at most 64 MiB of HBM per device.

v0:
```python
import functools

import jax
import jax.numpy as jnp
import numpy as np
from jax import lax
from jax.experimental import pallas as pl
from jax.experimental.pallas import tpu as pltpu
from jax.sharding import PartitionSpec as P

MESH = pl.DeviceIdType.MESH
WIDTH = 2048
TILES = 64
GROUPS = 8
STRIP = 32
OWN = 5
SLOTS = 32
TAPS = 8
BLOCKS = 16
ROWS = GROUPS * OWN * 2 * BLOCKS
PIECE = OWN * 2 * BLOCKS
BATCH = 256
F32 = jnp.float32
BF16 = jnp.bfloat16


def tables():
    turn = 2.0 * np.pi
    v = np.arange(TILES)[:, None]
    m = np.arange(128)[None, :]
    coarse = np.stack([np.cos(turn * (v * m % 64) / 64), np.sin(turn * (v * m % 64) / 64)])
    rows = np.arange(GROUPS * OWN)[:, None] * np.arange(WIDTH)[None, :] % WIDTH
    fine = np.zeros((GROUPS, 16, WIDTH))
    fine[:, 0:OWN] = np.cos(turn * rows / WIDTH).reshape(GROUPS, OWN, WIDTH)
    fine[:, 8 : 8 + OWN] = np.sin(turn * rows / WIDTH).reshape(GROUPS, OWN, WIDTH)
    q1 = np.arange(64)[:, None]
    u = np.arange(64)[None, :]
    cos64, sin64 = np.cos(turn * (q1 * u % 64) / 64), np.sin(turn * (q1 * u % 64) / 64)
    outer = np.block([[cos64, sin64], [-sin64, cos64]])
    l0 = np.arange(STRIP)
    twist = np.zeros((2, 64, 256))
    twist[0, :, : OWN * STRIP] = np.tile(np.cos(turn * (q1 * l0[None, :]) / WIDTH), (1, OWN))
    twist[1, :, : OWN * STRIP] = np.tile(np.sin(turn * (q1 * l0[None, :]) / WIDTH), (1, OWN))
    inner = np.zeros((2, 256, 2, 256))
    for e in range(2):
        for r in range(OWN):
            h = np.arange(BLOCKS)[:, None]
            angle = turn * ((2 * h + e) * l0[None, :] % 32) / 32
            c, s = np.cos(angle) / WIDTH, np.sin(angle) / WIDTH
            re = slice(r * 32, r * 32 + 16)
            im = slice(r * 32 + 16, r * 32 + 32)
            cols = slice(r * STRIP, (r + 1) * STRIP)
            inner[e, re, 0, cols] = c
            inner[e, re, 1, cols] = s
            inner[e, im, 1, cols] = c
            inner[e, im, 0, cols] = -s
    inner = inner.reshape(512, 512)
    f32 = lambda x: np.asarray(x, np.float32)
    bf16 = lambda x: jnp.asarray(f32(x)).astype(BF16)
    return f32(coarse), f32(fine), bf16(outer), bf16(outer.T), f32(twist), bf16(inner)


def kernel(
    image_ref,
    pay_ref,
    table_ref,
    coarse_ref,
    fine_hbm,
    outer_ref,
    outer_t_ref,
    twist_ref,
    inner_ref,
    back_ref,
    grad_ref,
    fine,
    basis,
    half_out,
    half_in,
    pay_in,
    fields,
    grid_all,
    windows,
    taps_v,
    taps_u,
    deposit,
    model,
    back_out,
    part_out,
    part_in,
    col_out,
    col_in,
    dirty_out,
    dirty_in,
    fine_sem,
    send_sem,
    recv_sem,
):
    u = lax.axis_index("uv")
    f = lax.axis_index("freq")

    fine_copy = pltpu.make_async_copy(fine_hbm.at[f], fine, fine_sem)
    fine_copy.start()
    barrier = pltpu.get_barrier_semaphore()

    def greet_uv(k, carry):
        peer = lax.rem(u + k, TILES)
        pl.semaphore_signal(barrier, inc=1, device_id=(peer, f), device_id_type=MESH)
        return carry

    def greet_freq(k, carry):
        peer = lax.rem(f + k, GROUPS)
        pl.semaphore_signal(barrier, inc=1, device_id=(u, peer), device_id_type=MESH)
        return carry

    lax.fori_loop(1, TILES, greet_uv, 0)
    lax.fori_loop(1, GROUPS, greet_freq, 0)

    def scatter_uv(src, dst, which):
        def step(k, carry):
            peer = lax.rem(u + k, TILES)
            pltpu.make_async_remote_copy(
                src_ref=src.at[peer],
                dst_ref=dst.at[u],
                send_sem=send_sem.at[which],
                recv_sem=recv_sem.at[which],
                device_id=(peer, f),
                device_id_type=MESH,
            ).start()
            return carry

        lax.fori_loop(1, TILES, step, 0)

    def scatter_freq(src_at, dst, which):
        def step(k, carry):
            peer = lax.rem(f + k, GROUPS)
            pltpu.make_async_remote_copy(
                src_ref=src_at(peer),
                dst_ref=dst.at[f],
                send_sem=send_sem.at[which],
                recv_sem=recv_sem.at[which],
                device_id=(u, peer),
                device_id_type=MESH,
            ).start()
            return carry

        lax.fori_loop(1, GROUPS, step, 0)

    def all_but_one(dst, which, count):
        blocks = dst.at[pl.ds(0, count - 1)]
        return pltpu.make_async_remote_copy(
            src_ref=blocks,
            dst_ref=blocks,
            send_sem=send_sem.at[which],
            recv_sem=recv_sem.at[which],
            device_id=(u, f),
            device_id_type=MESH,
        )

    fine_copy.wait()
    cos_a, sin_a = coarse_ref[0], coarse_ref[1]

    def make_basis(t, carry):
        lanes = pl.ds(pl.multiple_of(t * 128, 128), 128)
        for r in range(OWN):
            cos_b, sin_b = fine[r : r + 1, lanes], fine[8 + r : 9 + r, lanes]
            basis[r * 128 : r * 128 + 64, lanes] = (cos_a * cos_b - sin_a * sin_b).astype(BF16)
            basis[r * 128 + 64 : r * 128 + 128, lanes] = (
                -(sin_a * cos_b) - cos_a * sin_b
            ).astype(BF16)
        return carry

    lax.fori_loop(0, WIDTH // 128, make_basis, 0)

    half = lax.dot_general(
        basis[...], image_ref[...], (((1,), (1,)), ((), ())), preferred_element_type=F32
    )
    blank = jnp.zeros((2 * TILES, 256 - OWN * STRIP), F32)
    half = jnp.concatenate([half[r * 128 : (r + 1) * 128] for r in range(OWN)] + [blank], axis=1)
    half_out[...] = jnp.stack([half[:TILES], half[TILES:]], axis=1).astype(BF16)

    pl.semaphore_wait(barrier, TILES + GROUPS - 2)
    scatter_uv(half_out, half_in, 0)
    scatter_uv(pay_ref, pay_in, 1)
    half_in[pl.ds(u, 1)] = half_out[pl.ds(u, 1)]
    pay_in[pl.ds(u, 1)] = pay_ref[pl.ds(u, 1)]
    windows_zero = jnp.zeros((112, TILES * SLOTS), BF16)
    taps_v[144:256] = windows_zero

    all_but_one(half_in, 0, TILES).wait()
    half = half_in[...].astype(F32)
    half = jnp.concatenate([half[:, 0], half[:, 1]], axis=0).astype(BF16)
    mixed = jnp.dot(outer_ref[...], half, preferred_element_type=F32)
    real, imag = mixed[:64], mixed[64:]
    cos_t, sin_t = twist_ref[0], twist_ref[1]
    mixed = jnp.concatenate(
        [real * cos_t + imag * sin_t, imag * cos_t - real * sin_t], axis=1
    ).astype(BF16)
    own = lax.dot_general(
        inner_ref[...], mixed, (((1,), (1,)), ((), ())), preferred_element_type=F32
    )
    own = jnp.concatenate([own[:PIECE], own[256 : 256 + PIECE]], axis=1).astype(BF16)
    grid_all[pl.ds(f, 1)] = own[None]
    scatter_freq(lambda peer: grid_all.at[f], grid_all, 2)

    all_but_one(pay_in, 1, TILES).wait()
    arrived = pay_in[...].astype(F32)
    arrived = jnp.concatenate([arrived[:, 0], arrived[:, 1]], axis=1).T
    for k in range(8):
        fields[k] = jnp.concatenate(
            [arrived[k * 32 + 8 * g : k * 32 + 8 * g + 8] for g in range(4)], axis=1
        )
    table = table_ref[...]
    table_high = table.astype(BF16)
    table_low = (table - table_high.astype(F32)).astype(BF16)
    table_both = jnp.concatenate([table_high.astype(F32), table_low.astype(F32)], axis=0).astype(BF16)
    table_narrow = jnp.concatenate([table_high.astype(F32), jnp.zeros((8, 128), F32)], axis=0).astype(BF16)

    def prepare(i, carry):
        lanes = pl.ds(pl.multiple_of(i * BATCH, BATCH), BATCH)
        row, offset_u = fields[2, pl.ds(i, 1), :], fields[3, pl.ds(i, 1), :]
        low, offset_v = fields[5, pl.ds(i, 1), :], fields[6, pl.ds(i, 1), :]
        position = lax.broadcasted_iota(jnp.int32, (128, BATCH), 0).astype(F32)
        hot_u = jnp.where(position == offset_u, 1.0, 0.0).astype(BF16)
        hot_v = jnp.where(position == offset_v, 1.0, 0.0).astype(BF16)
        both = jnp.dot(table_both, hot_u, preferred_element_type=F32)
        factor_u = both[:8] + both[8:]
        factor_v = jnp.dot(table_narrow, hot_v, preferred_element_type=F32)
        away = lax.broadcasted_iota(jnp.int32, (144, BATCH), 0).astype(F32) - low
        across = jnp.zeros((144, BATCH), F32)
        for t in range(TAPS):
            across = jnp.where(away == t, factor_v[t : t + 1], across)
        taps_v[0:144, lanes] = across.astype(BF16)
        away = lax.broadcasted_iota(jnp.int32, (40, BATCH), 0).astype(F32) - row
        down = jnp.zeros((40, BATCH), F32)
        for t in range(TAPS):
            down = jnp.where(away == t, factor_u[t : t + 1], down)
        taps_u[i] = down
        return carry

    lax.fori_loop(0, TILES * SLOTS // BATCH, prepare, 0)

    all_but_one(grid_all, 2, GROUPS).wait()
    for g in range(GROUPS):
        piece = grid_all[g]
        windows[g * PIECE : (g + 1) * PIECE, 0:128] = piece
        piece = piece.astype(F32).reshape(OWN * 2, BLOCKS, 128)
        piece = jnp.concatenate([piece[:, 1:], piece[:, :1]], axis=1)
        windows[g * PIECE : (g + 1) * PIECE, 128:256] = piece.reshape(PIECE, 128).astype(BF16)

    def visit(i, carry):
        lanes = pl.ds(pl.multiple_of(i * BATCH, BATCH), BATCH)
        sampled = jnp.dot(windows[...], taps_v[:, lanes], preferred_element_type=F32)
        total = jnp.zeros((2 * BLOCKS, BATCH), F32)
        for r in range(GROUPS * OWN):
            total = total + sampled[r * 32 : (r + 1) * 32] * taps_u[i, r : r + 1, :]
        block = fields[4, pl.ds(i, 1), :]
        here = lax.broadcasted_iota(jnp.int32, (BLOCKS, BATCH), 0).astype(F32) == block
        parts = []
        for c in range(2):
            found = jnp.where(here, total[c * BLOCKS : (c + 1) * BLOCKS], 0.0)
            found = jnp.sum(found, axis=0, keepdims=True)
            model[c, pl.ds(i, 1), :] = found
            parts.append(jnp.where(here, fields[c, pl.ds(i, 1), :] - found, 0.0))
        left = jnp.concatenate(parts, axis=0)
        for r in range(GROUPS * OWN):
            deposit[r * 32 : (r + 1) * 32, lanes] = (left * taps_u[i, r : r + 1, :]).astype(BF16)
        return carry

    lax.fori_loop(0, TILES * SLOTS // BATCH, visit, 0)

    rows = []
    for c in range(2):
        values = model[c]
        for g in range(4):
            rows.append(values[:, 64 * g : 64 * g + 64])
    rows.append(jnp.zeros((64, 64), F32))
    back_out[...] = jnp.concatenate(rows, axis=0).T.reshape(TILES, 1, 128)
    scatter_uv(back_out, back_ref, 3)
    back_ref[pl.ds(u, 1)] = back_out[pl.ds(u, 1)]

    spread = lax.dot_general(
        deposit[...], taps_v[...], (((1,), (1,)), ((), ())), preferred_element_type=F32
    )
    for g in range(GROUPS):
        piece = spread[g * PIECE : (g + 1) * PIECE]
        over = piece[:, 128:256].reshape(OWN * 2, BLOCKS, 128)
        over = jnp.concatenate([over[:, BLOCKS - 1 :], over[:, : BLOCKS - 1]], axis=1)
        part_out[g] = (piece[:, 0:128] + over.reshape(PIECE, 128)).astype(BF16)
    scatter_freq(lambda peer: part_out.at[peer], part_in, 4)
    part_in[pl.ds(f, 1)] = part_out[pl.ds(f, 1)]
    all_but_one(part_in, 4, GROUPS).wait()
    whole = part_in[0].astype(F32)
    for g in range(1, GROUPS):
        whole = whole + part_in[g].astype(F32)

    whole = jnp.concatenate([whole, jnp.zeros((256 - PIECE, 128), F32)], axis=0).T
    whole = jnp.concatenate([whole[:64], whole[64:]], axis=1).astype(BF16)
    mixed = jnp.dot(whole, inner_ref[...], preferred_element_type=F32)
    real, imag = mixed[:, :256], mixed[:, 256:]
    mixed = jnp.concatenate(
        [real * cos_t - imag * sin_t, imag * cos_t + real * sin_t], axis=0
    ).astype(BF16)
    column = jnp.dot(outer_t_ref[...], mixed, preferred_element_type=F32)
    col_out[...] = jnp.stack([column[:TILES], column[TILES:]], axis=1).astype(BF16)
    scatter_uv(col_out, col_in, 5)
    col_in[pl.ds(u, 1)] = col_out[pl.ds(u, 1)]
    all_but_one(col_in, 5, TILES).wait()

    column = col_in[...].astype(F32)
    column = jnp.concatenate([column[:, 0], column[:, 1]], axis=0).T
    column = jnp.concatenate(
        [column[r * STRIP : (r + 1) * STRIP] for r in range(OWN)], axis=1
    ).astype(BF16)
    dirty = jnp.dot(column, basis[...], preferred_element_type=F32)
    for g in range(GROUPS):
        dirty_out[g] = dirty[:, g * 256 : (g + 1) * 256].astype(BF16)
    scatter_freq(lambda peer: dirty_out.at[peer], dirty_in, 6)
    dirty_in[pl.ds(f, 1)] = dirty_out[pl.ds(f, 1)]
    all_but_one(dirty_in, 6, GROUPS).wait()
    image = dirty_in[0].astype(F32)
    for g in range(1, GROUPS):
        image = image + dirty_in[g].astype(F32)
    grad_ref[...] = image
    all_but_one(back_ref, 3, TILES).wait()


def per_device(
    model_image, visibilities, cell_rows, cell_cols, kernel_offsets, slot_counts, kernel_table
):
    values = visibilities.reshape(2, TILES, SLOTS)
    cols = cell_cols.reshape(TILES, SLOTS)
    offsets = kernel_offsets.reshape(2, TILES, SLOTS)
    live = jnp.arange(SLOTS, dtype=jnp.int32)[None, :] < slot_counts.reshape(TILES, 1)
    first = [
        values[0],
        values[1],
        cell_rows.reshape(TILES, SLOTS).astype(F32),
        jnp.where(live, offsets[0], -1).astype(F32),
    ]
    second = [
        (cols // 128).astype(F32),
        (cols % 128).astype(F32),
        offsets[1].astype(F32),
        jnp.zeros((TILES, SLOTS), F32),
    ]
    payload = jnp.stack(
        [jnp.concatenate(first, axis=1), jnp.concatenate(second, axis=1)], axis=1
    ).astype(BF16)

    coarse, fine, outer, outer_t, twist, inner = tables()
    vmem = pl.BlockSpec(memory_space=pltpu.VMEM)
    count = TILES * SLOTS // BATCH
    back, gradient = pl.pallas_call(
        kernel,
        out_shape=(
            jax.ShapeDtypeStruct((TILES, 1, 128), F32),
            jax.ShapeDtypeStruct((STRIP, WIDTH // GROUPS), F32),
        ),
        in_specs=[vmem] * 4 + [pl.BlockSpec(memory_space=pl.ANY)] + [vmem] * 4,
        out_specs=(vmem, vmem),
        scratch_shapes=[
            pltpu.VMEM((16, WIDTH), F32),
            pltpu.VMEM((OWN * 128, WIDTH), BF16),
            pltpu.VMEM((TILES, 2, 256), BF16),
            pltpu.VMEM((TILES, 2, 256), BF16),
            pltpu.VMEM((TILES, 2, 128), BF16),
            pltpu.VMEM((8, count, BATCH), F32),
            pltpu.VMEM((GROUPS, PIECE, 128), BF16),
            pltpu.VMEM((ROWS, 256), BF16),
            pltpu.VMEM((256, TILES * SLOTS), BF16),
            pltpu.VMEM((count, GROUPS * OWN, BATCH), F32),
            pltpu.VMEM((ROWS, TILES * SLOTS), BF16),
            pltpu.VMEM((2, count, BATCH), F32),
            pltpu.VMEM((TILES, 1, 128), F32),
            pltpu.VMEM((GROUPS, PIECE, 128), BF16),
            pltpu.VMEM((GROUPS, PIECE, 128), BF16),
            pltpu.VMEM((TILES, 2, 256), BF16),
            pltpu.VMEM((TILES, 2, 256), BF16),
            pltpu.VMEM((GROUPS, STRIP, WIDTH // GROUPS), BF16),
            pltpu.VMEM((GROUPS, STRIP, WIDTH // GROUPS), BF16),
            pltpu.SemaphoreType.DMA,
            pltpu.SemaphoreType.DMA((7,)),
            pltpu.SemaphoreType.DMA((7,)),
        ],
        compiler_params=pltpu.CompilerParams(
            collective_id=0, has_side_effects=True, vmem_limit_bytes=48 << 20
        ),
    )(
        model_image,
        payload,
        kernel_table.T,
        jnp.asarray(coarse),
        jnp.asarray(fine),
        outer,
        outer_t,
        jnp.asarray(twist),
        inner,
    )
    sampled = back.reshape(TILES, 128)[:, : 2 * SLOTS].reshape(TILES, 2, SLOTS).transpose(1, 0, 2)
    residual = jnp.where(live[None], values - sampled, 0.0)
    return residual.reshape(2, 1, 1, TILES, SLOTS), gradient


def solution(mesh):
    placed = (
        P("uv", None),
        P(None, "uv", "freq", None, None),
        P("uv", "freq", None, None),
        P("uv", "freq", None, None),
        P(None, "uv", "freq", None, None),
        P("uv", "freq", None),
        P(),
    )
    return jax.shard_map(
        per_device,
        mesh=mesh,
        in_specs=placed,
        out_specs=(P(None, "uv", "freq", None, None), P("uv", "freq")),
        check_vma=False,
    )
```

profile of v0, /device:TPU:1, one launch (start us, length us, event | category | flops | bytes accessed | tf_op | source)
XLA Modules:
  0.0 74.1 jit_solution(12039527475695399268)
XLA Ops:
  0.6 0.0 copy-start.1
  0.6 0.8 %fusion.13 = (s32[1,1,1,64,32]{3,4,2,1,0:T(8,128)S(1)}, s32[1,1,1,64,32]{3,4,2,1,0:T(8,128)S(1)}) fusion(s32[2,1,1,64,32]{3,4,2,1,0:T(8,128)} %param.17), kind=kLoop, calls=%fused_computation.30 | loop fusion | bytes 32768 | tf_op jit(solution)/shard_map/slice | solution.py:338
  1.4 0.1 copy.42
  1.5 0.7 fusion.6
  2.3 0.9 %copy.33 = bf16[2,1,1,64,32]{4,3,2,1,0:T(8,128)(2,1)S(1)} copy(f32[2,1,1,64,32]{3,4,2,1,0:T(8,128)} %param.14) | data formatting | bytes 24576 | tf_op args[1]
  3.1 0.8 %copy.34 = s32[1,1,64,32]{3,2,1,0:T(8,128)S(1)} copy(s32[1,1,64,32]{2,3,1,0:T(8,128)} %param.15) | data formatting | bytes 16384 | tf_op args[2]
  3.9 0.1 maximum_bitcast_fusion
  4.1 0.0 copy-start.6
  4.1 0.1 copy.43
  4.2 0.0 copy-start.9
  4.2 0.0 copy-start.5
  4.2 0.7 copy-done.9
  4.9 0.0 copy-start.4
  4.9 0.1 copy.36
  5.0 0.0 copy-start.2
  5.0 0.0 copy-start.3
  5.0 0.1 pad.5.clone
  5.1 0.1 maximum_bitcast_fusion.1
  5.2 0.0 copy-start.7
  5.2 0.1 pad_maximum_fusion.pay_ref
  5.3 0.0 copy-done.1
  5.3 0.0 copy-done.6
  5.4 0.0 copy-done.5
  5.4 0.4 copy-done.4
  5.7 0.2 copy-done.2
  5.9 0.1 copy-done.3
  5.9 0.0 copy-done.7
  6.0 0.0 copy-start
  6.0 1.2 %copy-done = f32[8,16,2048]{2,1,0:T(8,128)S(1)} copy-done((f32[8,16,2048]{2,1,0:T(8,128)S(1)}, f32[8,16,2048]{2,1,0:T(8,128)}, u32[]{:S(2)}) %copy-start) | copy-done | bytes 1048600
  7.2 64.7 %shard_map.140 = (f32[64,1,128]{2,1,0:T(1,128)S(1)}, f32[32,256]{1,0:T(8,128)S(1)}) custom-call(bf16[32,2048]{1,0:T(8,128)(2,1)S(1)} %copy-done.2, bf16[64,2,128]{2,1,0:T(2,128)(2,1)S(1)} %pad_maximum_fusion.pay_ref, f32[8,128]{1,0:T(8,128)S(1)} %bitcast.62, f32[2,64,128]{2,1,0:T(8,128)S(1)} %copy-done.4, f32[8,16,2048]{2,1,0:T(8,128)S(1)} %copy-done, ...), custom_call_target="tpu_custom_call" | custom-call | tf_op jit(solution)/shard_map/pallas_call | solution.py:353
  71.9 0.0 copy-start.8
  71.9 0.1 copy.40
  72.0 0.0 copy-start.10
  72.0 0.7 copy-done.10
  72.6 0.1 iota_compare_fusion
  72.7 0.1 copy.32
  72.8 0.0 copy-done.8
  72.8 0.6 fusion.8
  73.4 0.6 copy.45
  (7 shorter events, 0.1 us)
Async XLA Ops:
  0.6 4.7 %copy-start.1 = (bf16[512,512]{1,0:T(8,128)(2,1)S(1)}, bf16[512,512]{1,0:T(8,128)(2,1)}, u32[]{:S(2)}) copy-start(bf16[512,512]{1,0:T(8,128)(2,1)} %constant.60.inner_ref) | copy-start | bytes 1572868
  4.1 1.3 %copy-start.6 = (bf16[128,128]{1,0:T(8,128)(2,1)S(1)}, bf16[128,128]{1,0:T(8,128)(2,1)}, u32[]{:S(2)}) copy-start(bf16[128,128]{1,0:T(8,128)(2,1)} %constant.59.outer_t_ref) | copy-start | bytes 98308
  4.2 0.7 copy-start.9
  4.2 1.2 %copy-start.5 = (bf16[128,128]{1,0:T(8,128)(2,1)S(1)}, bf16[128,128]{1,0:T(8,128)(2,1)}, u32[]{:S(2)}) copy-start(bf16[128,128]{1,0:T(8,128)(2,1)} %constant.58.outer_ref) | copy-start | bytes 98308
  4.9 0.8 %copy-start.4 = (f32[2,64,128]{2,1,0:T(8,128)S(1)}, f32[2,64,128]{2,1,0:T(8,128)}, u32[]{:S(2)}) copy-start(f32[2,64,128]{2,1,0:T(8,128)} %constant.49.clone.coarse_ref) | copy-start | bytes 196612
  5.0 0.9 %copy-start.2 = (bf16[32,2048]{1,0:T(8,128)(2,1)S(1)}, bf16[32,2048]{1,0:T(8,128)(2,1)}, u32[]{:S(2)}) copy-start(bf16[32,2048]{1,0:T(8,128)(2,1)} %image_ref.1) | copy-start | bytes 393220
  5.0 1.0 %copy-start.3 = (f32[2,64,256]{2,1,0:T(8,128)S(1)}, f32[2,64,256]{2,1,0:T(8,128)}, u32[]{:S(2)}) copy-start(f32[2,64,256]{2,1,0:T(8,128)} %constant.51.clone.twist_ref) | copy-start | bytes 393220
  5.2 0.7 copy-start.7
  6.0 1.2 %copy-start = (f32[8,16,2048]{2,1,0:T(8,128)S(1)}, f32[8,16,2048]{2,1,0:T(8,128)}, u32[]{:S(2)}) copy-start(f32[8,16,2048]{2,1,0:T(8,128)} %constant.50.clone.fine_hbm) | copy-start | bytes 3145732
  71.9 0.9 %copy-start.8 = (f32[2,1,1,64,32]{3,4,2,1,0:T(8,128)S(1)}, f32[2,1,1,64,32]{3,4,2,1,0:T(8,128)}, u32[]{:S(2)}) copy-start(f32[2,1,1,64,32]{3,4,2,1,0:T(8,128)} %param.14) | copy-start | bytes 49156
  72.0 0.7 copy-start.10
where the time goes:
time: 74.5 us; the launch traced here: 74.1 us
  Pallas kernels  64.7 us (87%)
  local copies, waits for them, and re-layouts  6.8 us (9%)
  other arithmetic  1.74 us (2%)
  between operations  0.81 us (1%)
    pallas_call x1, Pallas kernels, per_device(): pl.pallas_call(kernel, out_shape=(jax.ShapeDtypeStruct((TILES, 1, 128), F...  64.7 us
    unnamed x28, local copies, waits for them, and re-layouts  5.71 us

commit v1 on v0

v1 whole, which is shorter than its diff:
```python
import functools

import jax
import jax.numpy as jnp
import numpy as np
from jax import lax
from jax.experimental import pallas as pl
from jax.experimental.pallas import tpu as pltpu
from jax.sharding import PartitionSpec as P

MESH = pl.DeviceIdType.MESH
WIDTH = 2048
TILES = 64
GROUPS = 8
STRIP = 32
OWN = 5
SLOTS = 32
TAPS = 8
BLOCKS = 16
ROWS = GROUPS * OWN * 2 * BLOCKS
PIECE = OWN * 2 * BLOCKS
BATCH = 256
F32 = jnp.float32
BF16 = jnp.bfloat16


def tables():
    turn = 2.0 * np.pi
    v = np.arange(TILES)[:, None]
    m = np.arange(128)[None, :]
    coarse = np.stack([np.cos(turn * (v * m % 64) / 64), np.sin(turn * (v * m % 64) / 64)])
    rows = np.arange(GROUPS * OWN)[:, None] * np.arange(WIDTH)[None, :] % WIDTH
    fine = np.zeros((GROUPS, 16, WIDTH))
    fine[:, 0:OWN] = np.cos(turn * rows / WIDTH).reshape(GROUPS, OWN, WIDTH)
    fine[:, 8 : 8 + OWN] = np.sin(turn * rows / WIDTH).reshape(GROUPS, OWN, WIDTH)
    q1 = np.arange(64)[:, None]
    u = np.arange(64)[None, :]
    cos64, sin64 = np.cos(turn * (q1 * u % 64) / 64), np.sin(turn * (q1 * u % 64) / 64)
    outer = np.block([[cos64, sin64], [-sin64, cos64]])
    l0 = np.arange(STRIP)
    twist = np.zeros((2, 64, 256))
    twist[0, :, : OWN * STRIP] = np.tile(np.cos(turn * (q1 * l0[None, :]) / WIDTH), (1, OWN))
    twist[1, :, : OWN * STRIP] = np.tile(np.sin(turn * (q1 * l0[None, :]) / WIDTH), (1, OWN))
    inner = np.zeros((2, 256, 2, 256))
    for e in range(2):
        for r in range(OWN):
            h = np.arange(BLOCKS)[:, None]
            angle = turn * ((2 * h + e) * l0[None, :] % 32) / 32
            c, s = np.cos(angle) / WIDTH, np.sin(angle) / WIDTH
            re = slice(r * 32, r * 32 + 16)
            im = slice(r * 32 + 16, r * 32 + 32)
            cols = slice(r * STRIP, (r + 1) * STRIP)
            inner[e, re, 0, cols] = c
            inner[e, re, 1, cols] = s
            inner[e, im, 1, cols] = c
            inner[e, im, 0, cols] = -s
    inner = inner.reshape(512, 512)
    f32 = lambda x: np.asarray(x, np.float32)
    bf16 = lambda x: jnp.asarray(f32(x)).astype(BF16)
    return f32(coarse), f32(fine), bf16(outer), bf16(outer.T), f32(twist), bf16(inner)


def kernel(
    image_hbm,
    vis_hbm,
    rows_hbm,
    cols_hbm,
    offsets_hbm,
    counts_hbm,
    table_hbm,
    coarse_hbm,
    fine_hbm,
    outer_hbm,
    outer_t_hbm,
    twist_hbm,
    inner_hbm,
    residual_ref,
    grad_ref,
    image,
    vis,
    cell_rows,
    cell_cols,
    offsets,
    counts,
    table_in,
    coarse,
    fine,
    outer,
    outer_t,
    twist,
    inner,
    basis,
    half_out,
    half_in,
    pay_out,
    pay_in,
    fields,
    grid_all,
    windows,
    taps_v,
    taps_t,
    taps_u,
    totals,
    deposit,
    model,
    back_out,
    back_in,
    part_out,
    part_in,
    col_out,
    col_in,
    dirty_out,
    dirty_in,
    load_sem,
    send_sem,
    recv_sem,
    near_send,
    near_recv,
):
    u = lax.axis_index("uv")
    f = lax.axis_index("freq")
    chip, core = f // 2, lax.rem(f, 2)
    batches = TILES * SLOTS // BATCH

    loads = []
    for n, (source, target) in enumerate(
        [
            (image_hbm, image),
            (coarse_hbm, coarse),
            (fine_hbm.at[f], fine),
            (vis_hbm, vis),
            (rows_hbm, cell_rows),
            (cols_hbm, cell_cols),
            (offsets_hbm, offsets),
            (counts_hbm, counts),
            (table_hbm, table_in),
            (outer_hbm, outer),
            (twist_hbm, twist),
            (inner_hbm, inner),
            (outer_t_hbm, outer_t),
        ]
    ):
        load = pltpu.make_async_copy(source, target, load_sem.at[n])
        load.start()
        loads.append(load)
    barrier = pltpu.get_barrier_semaphore()

    def peer_uv(j):
        away = (j + 1) // 2
        return lax.rem(u + TILES // 2 + away * (2 * lax.rem(j, 2) - 1) + TILES, TILES)

    def greet_uv(j, carry):
        pl.semaphore_signal(barrier, inc=1, device_id=(peer_uv(j), f), device_id_type=MESH)
        return carry

    lax.fori_loop(0, TILES - 1, greet_uv, 0)

    def at(dx, dc):
        return 2 * lax.rem(chip + dx, 4) + lax.rem(core + dc, 2)

    for dx in (2, 1, 3, 0):
        for dc in (0, 1):
            if dx or dc:
                pl.semaphore_signal(
                    barrier, inc=1, device_id=(u, at(dx, dc)), device_id_type=MESH
                )

    def scatter_uv(src, dst, which):
        def step(j, carry):
            peer = peer_uv(j)
            pltpu.make_async_remote_copy(
                src_ref=src.at[peer],
                dst_ref=dst.at[u],
                send_sem=send_sem.at[which],
                recv_sem=recv_sem.at[which],
                device_id=(peer, f),
                device_id_type=MESH,
            ).start()
            return carry

        lax.fori_loop(0, TILES - 1, step, 0)

    def all_but_one(dst, which):
        blocks = dst.at[pl.ds(0, TILES - 1)]
        return pltpu.make_async_remote_copy(
            src_ref=blocks,
            dst_ref=blocks,
            send_sem=send_sem.at[which],
            recv_sem=recv_sem.at[which],
            device_id=(u, f),
            device_id_type=MESH,
        )

    def send_near(src, dst, which, dx, dc):
        copy = pltpu.make_async_remote_copy(
            src_ref=src,
            dst_ref=dst.at[f],
            send_sem=near_send.at[which, 2 * dx + dc],
            recv_sem=near_recv.at[which, 2 * dx + dc],
            device_id=(u, at(dx, dc)),
            device_id_type=MESH,
        )
        copy.start()
        return copy

    for n in range(3):
        loads[n].wait()
    cos_a, sin_a = coarse[0], coarse[1]

    def make_basis(t, carry):
        lanes = pl.ds(pl.multiple_of(t * 128, 128), 128)
        for r in range(OWN):
            cos_b, sin_b = fine[r : r + 1, lanes], fine[8 + r : 9 + r, lanes]
            basis[r * 128 : r * 128 + 64, lanes] = (cos_a * cos_b - sin_a * sin_b).astype(BF16)
            basis[r * 128 + 64 : r * 128 + 128, lanes] = (
                -(sin_a * cos_b) - cos_a * sin_b
            ).astype(BF16)
        return carry

    lax.fori_loop(0, WIDTH // 128, make_basis, 0)
    half = lax.dot_general(
        basis[...], image[...], (((1,), (1,)), ((), ())), preferred_element_type=F32
    )
    blank = jnp.zeros((2 * TILES, 256 - OWN * STRIP), F32)
    half = jnp.concatenate([half[r * 128 : (r + 1) * 128] for r in range(OWN)] + [blank], axis=1)
    half_out[...] = jnp.stack([half[:TILES], half[TILES:]], axis=1).astype(BF16)

    for n in range(3, len(loads)):
        loads[n].wait()
    slot = lax.broadcasted_iota(jnp.int32, (SLOTS, TILES), 0)
    live = slot < counts[...]
    cols = cell_cols[...]
    high = lax.shift_right_logical(cols, 7)
    packed = jnp.concatenate(
        [
            vis[0],
            vis[1],
            cell_rows[...].astype(F32),
            jnp.where(live, offsets[0], -1).astype(F32),
            high.astype(F32),
            (cols - high * 128).astype(F32),
            offsets[1].astype(F32),
            jnp.zeros((SLOTS, TILES), F32),
        ],
        axis=0,
    ).T
    pay_out[...] = jnp.stack([packed[:, :128], packed[:, 128:]], axis=1).astype(BF16)

    pl.semaphore_wait(barrier, TILES + GROUPS - 2)
    scatter_uv(half_out, half_in, 0)
    scatter_uv(pay_out, pay_in, 1)
    half_in[pl.ds(u, 1)] = half_out[pl.ds(u, 1)]
    pay_in[pl.ds(u, 1)] = pay_out[pl.ds(u, 1)]
    taps_v[144:256] = jnp.zeros((112, TILES * SLOTS), BF16)
    totals[...] = jnp.zeros_like(totals)

    all_but_one(half_in, 0).wait()
    half = half_in[...].astype(F32)
    half = jnp.concatenate([half[:, 0], half[:, 1]], axis=0).astype(BF16)
    mixed = jnp.dot(outer[...], half, preferred_element_type=F32)
    real, imag = mixed[:64], mixed[64:]
    cos_t, sin_t = twist[0], twist[1]
    mixed = jnp.concatenate(
        [real * cos_t + imag * sin_t, imag * cos_t - real * sin_t], axis=1
    ).astype(BF16)
    own = lax.dot_general(
        inner[...], mixed, (((1,), (1,)), ((), ())), preferred_element_type=F32
    )
    own = jnp.concatenate([own[:PIECE], own[256 : 256 + PIECE]], axis=1).astype(BF16)
    grid_all[pl.ds(f, 1)] = own[None]
    pieces = {}
    for dx in (2, 1, 3, 0):
        for dc in (0, 1):
            if dx or dc:
                pieces[dx, dc] = send_near(grid_all.at[f], grid_all, 0, dx, dc)

    all_but_one(pay_in, 1).wait()
    arrived = pay_in[...].astype(F32)
    arrived = jnp.concatenate([arrived[:, 0], arrived[:, 1]], axis=1).T
    for k in range(8):
        fields[k] = jnp.concatenate(
            [arrived[k * 32 + 8 * g : k * 32 + 8 * g + 8] for g in range(4)], axis=1
        )
    table = table_in[...]
    table_high = table.astype(BF16)
    table_low = (table - table_high.astype(F32)).astype(BF16)
    table_both = jnp.concatenate([table_high.astype(F32), table_low.astype(F32)], axis=0).astype(BF16)
    table_narrow = jnp.concatenate([table_high.astype(F32), jnp.zeros((8, 128), F32)], axis=0).astype(BF16)

    def prepare(i, carry):
        lanes = pl.ds(pl.multiple_of(i * BATCH, BATCH), BATCH)
        row, offset_u = fields[2, pl.ds(i, 1), :], fields[3, pl.ds(i, 1), :]
        low, offset_v = fields[5, pl.ds(i, 1), :], fields[6, pl.ds(i, 1), :]
        position = lax.broadcasted_iota(jnp.int32, (128, BATCH), 0).astype(F32)
        hot_u = jnp.where(position == offset_u, 1.0, 0.0).astype(BF16)
        hot_v = jnp.where(position == offset_v, 1.0, 0.0).astype(BF16)
        both = jnp.dot(table_both, hot_u, preferred_element_type=F32)
        factor_u = both[:8] + both[8:]
        factor_v = jnp.dot(table_narrow, hot_v, preferred_element_type=F32)
        away = lax.broadcasted_iota(jnp.int32, (144, BATCH), 0).astype(F32) - low
        across = jnp.zeros((144, BATCH), F32)
        for t in range(TAPS):
            across = jnp.where(away == t, factor_v[t : t + 1], across)
        taps_v[0:144, lanes] = across.astype(BF16)
        across = jnp.concatenate([across, jnp.zeros((112, BATCH), F32)], axis=0)
        taps_t[lanes, :] = across.T.astype(BF16)
        place = lax.broadcasted_iota(jnp.int32, (64, BATCH), 0)
        group = lax.shift_right_logical(place, 3)
        away = (group * OWN + place - group * 8).astype(F32) - row
        down = jnp.zeros((64, BATCH), F32)
        for t in range(TAPS):
            down = jnp.where(away == t, factor_u[t : t + 1], down)
        taps_u[i] = down.reshape(GROUPS, 8, BATCH)
        return carry

    lax.fori_loop(0, batches, prepare, 0)

    for dx in (0, 1, 3, 2):
        there = lax.rem(chip - dx + 4, 4)
        for dc in (0, 1):
            if dx or dc:
                pieces[dx, dc].wait_recv()
        for side in range(2):
            lines = pl.ds(side * PIECE, PIECE)
            piece = grid_all[pl.ds(2 * there + side, 1)].reshape(PIECE, 128)
            windows[there, lines, 0:128] = piece
            piece = piece.astype(F32).reshape(OWN * 2, BLOCKS, 128)
            piece = jnp.concatenate([piece[:, 1:], piece[:, :1]], axis=1)
            windows[there, lines, 128:256] = piece.reshape(PIECE, 128).astype(BF16)

        def sample(i, carry):
            lanes = pl.ds(pl.multiple_of(i * BATCH, BATCH), BATCH)
            sampled = jnp.dot(windows[there], taps_v[:, lanes], preferred_element_type=F32)
            total = totals[i]
            for side in range(2):
                taps = taps_u[i, pl.ds(2 * there + side, 1)].reshape(8, BATCH)
                for r in range(OWN):
                    n = (side * OWN + r) * 32
                    total = total + sampled[n : n + 32] * taps[r : r + 1]
            totals[i] = total
            return carry

        lax.fori_loop(0, batches, sample, 0)

    def visit(i, carry):
        lanes = pl.ds(pl.multiple_of(i * BATCH, BATCH), BATCH)
        block = fields[4, pl.ds(i, 1), :]
        here = lax.broadcasted_iota(jnp.int32, (BLOCKS, BATCH), 0).astype(F32) == block
        parts = []
        for c in range(2):
            found = jnp.where(here, totals[i, c * BLOCKS : (c + 1) * BLOCKS], 0.0)
            found = jnp.sum(found, axis=0, keepdims=True)
            model[c, pl.ds(i, 1), :] = found
            parts.append(jnp.where(here, fields[c, pl.ds(i, 1), :] - found, 0.0))
        left = jnp.concatenate(parts, axis=0)
        for g in range(GROUPS):
            taps = taps_u[i, g]
            for r in range(OWN):
                n = (g % 2 * OWN + r) * 32
                deposit[g // 2, n : n + 32, lanes] = (left * taps[r : r + 1]).astype(BF16)
        return carry

    lax.fori_loop(0, batches, visit, 0)

    sums = {}
    for dx in (2, 1, 3, 0):
        there = lax.rem(chip + dx, 4)
        spread = jnp.dot(deposit[there], taps_t[...], preferred_element_type=F32)
        for side in range(2):
            piece = spread[side * PIECE : (side + 1) * PIECE]
            over = piece[:, 128:256].reshape(OWN * 2, BLOCKS, 128)
            over = jnp.concatenate([over[:, BLOCKS - 1 :], over[:, : BLOCKS - 1]], axis=1)
            piece = (piece[:, 0:128] + over.reshape(PIECE, 128)).astype(BF16)
            part_out[pl.ds(2 * there + side, 1)] = piece[None]
        for dc in (0, 1):
            if dx or dc:
                sums[dx, dc] = send_near(part_out.at[at(dx, dc)], part_in, 1, dx, dc)
    part_in[pl.ds(f, 1)] = part_out[pl.ds(f, 1)]

    lines = []
    for c in range(2):
        values = model[c]
        for g in range(4):
            lines.append(values[:, 64 * g : 64 * g + 64])
    lines.append(jnp.zeros((64, 64), F32))
    back_out[...] = jnp.concatenate(lines, axis=0).T.reshape(TILES, 1, 128)
    scatter_uv(back_out, back_in, 2)
    back_in[pl.ds(u, 1)] = back_out[pl.ds(u, 1)]

    for copy in sums.values():
        copy.wait_recv()
    whole = part_in[0].astype(F32)
    for g in range(1, GROUPS):
        whole = whole + part_in[g].astype(F32)

    whole = jnp.concatenate([whole, jnp.zeros((256 - PIECE, 128), F32)], axis=0).T
    whole = jnp.concatenate([whole[:64], whole[64:]], axis=1).astype(BF16)
    mixed = jnp.dot(whole, inner[...], preferred_element_type=F32)
    real, imag = mixed[:, :256], mixed[:, 256:]
    mixed = jnp.concatenate(
        [real * cos_t - imag * sin_t, imag * cos_t + real * sin_t], axis=0
    ).astype(BF16)
    column = jnp.dot(outer_t[...], mixed, preferred_element_type=F32)
    col_out[...] = jnp.stack([column[:TILES], column[TILES:]], axis=1).astype(BF16)
    scatter_uv(col_out, col_in, 3)
    col_in[pl.ds(u, 1)] = col_out[pl.ds(u, 1)]

    all_but_one(back_in, 2).wait()
    sampled = back_in[...].reshape(TILES, 128).T
    for c in range(2):
        residual_ref[c] = jnp.where(
            slot < counts[...], vis[c] - sampled[c * SLOTS : (c + 1) * SLOTS], 0.0
        )
    for copies in (pieces, sums):
        for copy in copies.values():
            copy.wait_send()

    all_but_one(col_in, 3).wait()
    column = col_in[...].astype(F32)
    column = jnp.concatenate([column[:, 0], column[:, 1]], axis=0).T
    column = jnp.concatenate(
        [column[r * STRIP : (r + 1) * STRIP] for r in range(OWN)], axis=1
    ).astype(BF16)
    shares = {}
    for dx in (2, 1, 3, 0):
        there = lax.rem(chip + dx, 4)
        lanes = pl.ds(pl.multiple_of(there * 512, 512), 512)
        dirty = jnp.dot(column, basis[:, lanes], preferred_element_type=F32)
        for side in range(2):
            piece = dirty[:, side * 256 : (side + 1) * 256].astype(BF16)
            dirty_out[pl.ds(2 * there + side, 1)] = piece[None]
        for dc in (0, 1):
            if dx or dc:
                shares[dx, dc] = send_near(dirty_out.at[at(dx, dc)], dirty_in, 2, dx, dc)
    dirty_in[pl.ds(f, 1)] = dirty_out[pl.ds(f, 1)]
    for copy in shares.values():
        copy.wait()
    picture = dirty_in[0].astype(F32)
    for g in range(1, GROUPS):
        picture = picture + dirty_in[g].astype(F32)
    grad_ref[...] = picture


def per_device(
    model_image, visibilities, cell_rows, cell_cols, kernel_offsets, slot_counts, kernel_table
):
    constants = [jnp.asarray(x) for x in tables()]
    inputs = [
        model_image,
        visibilities.reshape(2, TILES, SLOTS).transpose(0, 2, 1),
        cell_rows.reshape(TILES, SLOTS).T,
        cell_cols.reshape(TILES, SLOTS).T,
        kernel_offsets.reshape(2, TILES, SLOTS).transpose(0, 2, 1),
        slot_counts.reshape(1, TILES),
        kernel_table.T,
    ] + constants
    vmem = pl.BlockSpec(memory_space=pltpu.VMEM)
    hbm = pl.BlockSpec(memory_space=pltpu.HBM)
    batches = TILES * SLOTS // BATCH
    local = [pltpu.VMEM(x.shape[1:] if n == 8 else x.shape, x.dtype) for n, x in enumerate(inputs)]
    residual, gradient = pl.pallas_call(
        kernel,
        out_shape=(
            jax.ShapeDtypeStruct((2, SLOTS, TILES), F32),
            jax.ShapeDtypeStruct((STRIP, WIDTH // GROUPS), F32),
        ),
        in_specs=[hbm] * len(inputs),
        out_specs=(vmem, vmem),
        scratch_shapes=local
        + [
            pltpu.VMEM((OWN * 128, WIDTH), BF16),
            pltpu.VMEM((TILES, 2, 256), BF16),
            pltpu.VMEM((TILES, 2, 256), BF16),
            pltpu.VMEM((TILES, 2, 128), BF16),
            pltpu.VMEM((TILES, 2, 128), BF16),
            pltpu.VMEM((8, batches, BATCH), F32),
            pltpu.VMEM((GROUPS, PIECE, 128), BF16),
            pltpu.VMEM((4, 2 * PIECE, 256), BF16),
            pltpu.VMEM((256, TILES * SLOTS), BF16),
            pltpu.VMEM((TILES * SLOTS, 256), BF16),
            pltpu.VMEM((batches, GROUPS, 8, BATCH), F32),
            pltpu.VMEM((batches, 2 * BLOCKS, BATCH), F32),
            pltpu.VMEM((4, 2 * PIECE, TILES * SLOTS), BF16),
            pltpu.VMEM((2, batches, BATCH), F32),
            pltpu.VMEM((TILES, 1, 128), F32),
            pltpu.VMEM((TILES, 1, 128), F32),
            pltpu.VMEM((GROUPS, PIECE, 128), BF16),
            pltpu.VMEM((GROUPS, PIECE, 128), BF16),
            pltpu.VMEM((TILES, 2, 256), BF16),
            pltpu.VMEM((TILES, 2, 256), BF16),
            pltpu.VMEM((GROUPS, STRIP, WIDTH // GROUPS), BF16),
            pltpu.VMEM((GROUPS, STRIP, WIDTH // GROUPS), BF16),
            pltpu.SemaphoreType.DMA((len(inputs),)),
            pltpu.SemaphoreType.DMA((4,)),
            pltpu.SemaphoreType.DMA((4,)),
            pltpu.SemaphoreType.DMA((3, GROUPS)),
            pltpu.SemaphoreType.DMA((3, GROUPS)),
        ],
        compiler_params=pltpu.CompilerParams(
            collective_id=0, has_side_effects=True, vmem_limit_bytes=60 << 20
        ),
    )(*inputs)
    return residual.transpose(0, 2, 1).reshape(2, 1, 1, TILES, SLOTS), gradient


def solution(mesh):
    placed = (
        P("uv", None),
        P(None, "uv", "freq", None, None),
        P("uv", "freq", None, None),
        P("uv", "freq", None, None),
        P(None, "uv", "freq", None, None),
        P("uv", "freq", None),
        P(),
    )
    return jax.shard_map(
        per_device,
        mesh=mesh,
        in_specs=placed,
        out_specs=(P(None, "uv", "freq", None, None), P("uv", "freq")),
        check_vma=False,
    )
```

time: 74.5 us -> 63.5 us (0.85)
  local copies, waits for them, and re-layouts: 6.8 us -> 2 us
  Pallas kernels: 64.7 us -> 60.7 us
  other arithmetic: 1.74 us -> 0 us
    pallas_call x1, Pallas kernels: 64.7 us -> 60.7 us  [per_device(): pl.pallas_call(kernel, out_shape=(jax.ShapeDtypeStruct((2, SLOTS, TILES),...]
    unnamed x28 -> x4, local copies, waits for them, and re-layouts: 5.71 us -> 2 us
    another operation x5 -> x0, other arithmetic: 1.03 us -> none
    slice x2 -> x0, local copies, waits for them, and re-layouts: 0.87 us -> none  [the longest x1 0.79 us: per_device(): offsets[0]]
where the time goes in v1:
time: 63.5 us; the launch traced here: 63.3 us
  Pallas kernels  60.7 us (96%)
  local copies, waits for them, and re-layouts  2 us (3%)
  between operations  0.65 us (1%)
    pallas_call x1, Pallas kernels, per_device(): pl.pallas_call(kernel, out_shape=(jax.ShapeDtypeStruct((2, SLOTS, TILES),...  60.7 us
    unnamed x4, local copies, waits for them, and re-layouts  2 us

profile of v1, /device:TPU:1, one launch (start us, length us, event | category | flops | bytes accessed | tf_op | source)
XLA Modules:
  0.0 63.3 jit_solution(5435687034451973513)
XLA Ops:
  0.6 60.7 %shard_map.140 = (f32[2,32,64]{2,1,0:T(8,128)}, f32[32,256]{1,0:T(8,128)}) custom-call(bf16[32,2048]{1,0:T(8,128)(2,1)} %image_hbm.1, f32[2,32,64]{2,1,0:T(8,128)} %bitcast.19, s32[32,64]{1,0:T(8,128)} %bitcast.22, s32[32,64]{1,0:T(8,128)} %bitcast.23, s32[2,32,64]{2,1,0:T(8,128)} %bitcast.20, s32[1,64]{1,0:T(1,128)} %bitcast.25, f32[8,128]{1,0:T(8,128)} %bitcast.24, ...), custom_call_target="tpu_custom_call" | custom-call | tf_op jit(solution)/shard_map/pallas_call | solution.py:461
  61.3 0.0 copy-start
  61.3 1.4 %copy.18 = f32[2,1,1,64,32]{3,4,2,1,0:T(8,128)} copy(f32[2,1,1,64,32]{3,4,2,1,0:T(8,128)} %bitcast.21) | data formatting | bytes 32768
  62.7 0.0 copy-done
  62.7 0.6 copy.19
Async XLA Ops:
  61.3 1.4 %copy-start = (f32[32,256]{1,0:T(8,128)S(1)}, f32[32,256]{1,0:T(8,128)}, u32[]{:S(2)}) copy-start(f32[32,256]{1,0:T(8,128)} %get-tuple-element.11) | copy-start | bytes 98308

commit v2 on v1

--- a/solution.py
+++ b/solution.py
@@ -217,7 +217,7 @@
             ).astype(BF16)
         return carry
 
-    lax.fori_loop(0, WIDTH // 128, make_basis, 0)
+    lax.fori_loop(0, WIDTH // 128, make_basis, 0, unroll=2)
     half = lax.dot_general(
         basis[...], image[...], (((1,), (1,)), ((), ())), preferred_element_type=F32
     )
@@ -313,7 +313,7 @@
         taps_u[i] = down.reshape(GROUPS, 8, BATCH)
         return carry
 
-    lax.fori_loop(0, batches, prepare, 0)
+    lax.fori_loop(0, batches, prepare, 0, unroll=4)
 
     for dx in (0, 1, 3, 2):
         there = lax.rem(chip - dx + 4, 4)
@@ -340,7 +340,7 @@
             totals[i] = total
             return carry
 
-        lax.fori_loop(0, batches, sample, 0)
+        lax.fori_loop(0, batches, sample, 0, unroll=batches)
 
     def visit(i, carry):
         lanes = pl.ds(pl.multiple_of(i * BATCH, BATCH), BATCH)
@@ -360,7 +360,7 @@
                 deposit[g // 2, n : n + 32, lanes] = (left * taps[r : r + 1]).astype(BF16)
         return carry
 
-    lax.fori_loop(0, batches, visit, 0)
+    lax.fori_loop(0, batches, visit, 0, unroll=batches)
 
     sums = {}
     for dx in (2, 1, 3, 0):
@@ -441,6 +441,17 @@
     grad_ref[...] = picture
 
 
+def publish(residual_ref, grad_ref, residual_hbm, grad_hbm, sems):
+    copies = [
+        pltpu.make_async_copy(residual_ref, residual_hbm, sems.at[0]),
+        pltpu.make_async_copy(grad_ref, grad_hbm, sems.at[1]),
+    ]
+    for copy in copies:
+        copy.start()
+    for copy in copies:
+        copy.wait()
+
+
 def per_device(
     model_image, visibilities, cell_rows, cell_cols, kernel_offsets, slot_counts, kernel_table
 ):
@@ -461,8 +472,8 @@
     residual, gradient = pl.pallas_call(
         kernel,
         out_shape=(
-            jax.ShapeDtypeStruct((2, SLOTS, TILES), F32),
-            jax.ShapeDtypeStruct((STRIP, WIDTH // GROUPS), F32),
+            pltpu.VMEM((2, SLOTS, TILES), F32),
+            pltpu.VMEM((STRIP, WIDTH // GROUPS), F32),
         ),
         in_specs=[hbm] * len(inputs),
         out_specs=(vmem, vmem),
@@ -497,9 +508,20 @@
             pltpu.SemaphoreType.DMA((3, GROUPS)),
         ],
         compiler_params=pltpu.CompilerParams(
-            collective_id=0, has_side_effects=True, vmem_limit_bytes=60 << 20
+            collective_id=0, has_side_effects=True, vmem_limit_bytes=40 << 20
         ),
-    )(*inputs)
+    )(*[pltpu.with_memory_space_constraint(x, pltpu.HBM) for x in inputs])
+    residual, gradient = pl.pallas_call(
+        publish,
+        out_shape=(
+            jax.ShapeDtypeStruct((2, SLOTS, TILES), F32),
+            jax.ShapeDtypeStruct((STRIP, WIDTH // GROUPS), F32),
+        ),
+        in_specs=[vmem] * 2,
+        out_specs=(hbm, hbm),
+        scratch_shapes=[pltpu.SemaphoreType.DMA((2,))],
+        compiler_params=pltpu.CompilerParams(vmem_limit_bytes=1 << 20),
+    )(residual, gradient)
     return residual.transpose(0, 2, 1).reshape(2, 1, 1, TILES, SLOTS), gradient
 
 

time: 63.5 us -> 57.4 us (0.904)
  Pallas kernels: 60.7 us -> 56.7 us
  local copies, waits for them, and re-layouts: 2 us -> 0 us
    pallas_call x1 -> x2, Pallas kernels: 60.7 us -> 56.7 us  [the longest x1 56 us: per_device(): pl.pallas_call(kernel, out_shape=(pltpu.VMEM((2, SLOTS, TILES), F32), plt...]
    unnamed x4 -> x0, local copies, waits for them, and re-layouts: 2 us -> none
where the time goes in v2:
time: 57.4 us; the launch traced here: 57.3 us
  Pallas kernels  56.7 us (99%)
  between operations  0.64 us (1%)
    pallas_call x1, Pallas kernels, per_device(): pl.pallas_call(kernel, out_shape=(pltpu.VMEM((2, SLOTS, TILES), F32), plt...  56 us

profile of v2, /device:TPU:1, one launch (start us, length us, event | category | flops | bytes accessed | tf_op | source)
XLA Modules:
  0.0 57.3 jit_solution(3074123518190215097)
XLA Ops:
  0.6 56.0 %shard_map.140 = (f32[2,32,64]{2,1,0:T(8,128)S(1)}, f32[32,256]{1,0:T(8,128)S(1)}) custom-call(bf16[32,2048]{1,0:T(8,128)(2,1)} %image_hbm.1, f32[2,32,64]{2,1,0:T(8,128)} %bitcast.19, s32[32,64]{1,0:T(8,128)} %bitcast.21, s32[32,64]{1,0:T(8,128)} %bitcast.22, s32[2,32,64]{2,1,0:T(8,128)} %bitcast.20, s32[1,64]{1,0:T(1,128)} %bitcast.24, f32[8,128]{1,0:T(8,128)} %bitcast.23, ...), custom_call_target="tpu_custom_call" | custom-call | tf_op jit(solution)/shard_map/pallas_call | solution.py:472
  56.7 0.6 %shard_map.141 = (f32[2,32,64]{2,1,0:T(8,128)}, f32[32,256]{1,0:T(8,128)}) custom-call(f32[2,32,64]{2,1,0:T(8,128)S(1)} %get-tuple-element.6.residual_ref, f32[32,256]{1,0:T(8,128)S(1)} %get-tuple-element.7.grad_ref), custom_call_target="tpu_custom_call" | custom-call | tf_op jit(solution)/shard_map/pallas_call | solution.py:514
